TPU v7x, 32 devices: a whole 2x2x4 slice. The times are simulated.
32 devices in a mesh: space: 8 (over z, x), field: 4 (over y, core).
Axes of the slice: x: 2, y: 2, z: 4, core: 2. Of those that a mesh axis runs over, the one named last changes fastest.
Arguments:
- composition_vector: float32 [4, 32, 32, 16, 128], P('field', None, 'space'), may hold values from -6 to 6
- filtered_motion: float32 [3, 32, 16, 128], P(None, 'space', 'field'), may hold values from -1.8 to 1.8
- spreading_strength: float32 [32, 16, 128], P('space', 'field'), may hold values from 0.02 to 0.12
- blend_relax_multiplier: float32 [32, 16, 128], P('space', 'field'), may hold values from 0.2 to 0.9
- thermal_level: float32 [32, 16, 128], P('space', 'field'), may hold values from 0.5 to 2
- brownian_jumps: float32 [2, 4, 3], P(None, 'field'), may hold values from -2.5 to 2.5
- left_bilinear_weights: bfloat16 [206, 32], replicated, may hold values from -1 to 1
- right_bilinear_weights: bfloat16 [206, 32], replicated, may hold values from -1 to 1
- species_yield_weights: bfloat16 [32, 206], replicated, may hold values from -0.4375 to 0.4375
- arrhenius_prefactor: float32 [206], replicated, may hold values from 0.3 to 3
- ignition_energy_ratio: float32 [206], replicated, may hold values from 0.2 to 2
Outputs:
- result: float32 [4, 32, 32, 16, 128], P('field', None, 'space')
All inputs are finite; a program needn't handle non-finite values.
Results may differ from a plain program's by a relative error of at most 0.00068.
Values sent between devices are 32-bit elements; how exact they have to be, the bound alone decides.
A program may use at most 64 MiB of HBM per device.

v0:
```python
import jax
import jax.numpy as jnp
from jax import lax
from jax.sharding import PartitionSpec as P

STEPS = 2
SUB = 5


chem_step = 0.2


def extended(value, sides, width):
    for axis, dim in sides:
        count, length = (lax.axis_size(axis), value.shape[dim])
        up = [(i, (i + 1) % count) for i in range(count)]
        down = [(j, i) for i, j in up]
        last = lax.slice_in_dim(value, length - width, length, axis=dim)
        leading = lax.slice_in_dim(value, 0, width, axis=dim)
        before = lax.ppermute(last, axis, up)
        after = lax.ppermute(leading, axis, down)
        value = jnp.concatenate([before, value, after], axis=dim)
    return value


def transport(padded, current, mean, filtered_motion, spreading_strength, mixing, wiener):
    x_plus = padded[:, 2:]
    x_minus = padded[:, :-2]
    y_plus = jnp.roll(current, -1, 2)
    y_minus = jnp.roll(current, 1, 2)
    z_plus = jnp.roll(current, -1, 3)
    z_minus = jnp.roll(current, 1, 3)
    grad_x = 0.5 * (x_plus - x_minus)
    grad_y = 0.5 * (y_plus - y_minus)
    grad_z = 0.5 * (z_plus - z_minus)
    laplace = x_plus + x_minus + y_plus + y_minus + z_plus + z_minus - 6.0 * current
    advect = filtered_motion[0] * grad_x + filtered_motion[1] * grad_y + filtered_motion[2] * grad_z
    noise = jnp.sqrt(2.0 * spreading_strength) * (
        wiener[0] * grad_x + wiener[1] * grad_y + wiener[2] * grad_z
    )
    return current - advect + spreading_strength * laplace + noise - mixing * (current - mean)


def react(block, arrhenius, left_bilinear_weights, right_bilinear_weights, species_yield_weights):
    for substep in range(SUB):
        lowered = block.astype(jnp.bfloat16)
        forward = jnp.dot(left_bilinear_weights, lowered, preferred_element_type=jnp.float32)
        backward = jnp.dot(right_bilinear_weights, lowered, preferred_element_type=jnp.float32)
        saturation = 1.0 + forward * forward + backward * backward
        rates = (arrhenius * forward * backward / saturation).astype(jnp.bfloat16)
        block = block + chem_step * jnp.dot(
            species_yield_weights, rates, preferred_element_type=jnp.float32
        )
    return block


def kinetic_yield_term(
    carried_ensemble,
    thermal_level,
    arrhenius_prefactor,
    ignition_energy_ratio,
    left_bilinear_weights,
    right_bilinear_weights,
    species_yield_weights,
):
    species_count, planes, vertical_extent, streamwise_extent = carried_ensemble.shape

    def one_plane(plane_index, current):
        starting_ensemble = jnp.asarray(plane_index).astype(jnp.int32)
        block = lax.dynamic_slice_in_dim(current, starting_ensemble, 1, 1).reshape(
            species_count, vertical_extent * streamwise_extent
        )
        enthalpy_output = lax.dynamic_slice_in_dim(thermal_level, starting_ensemble, 1, 0).reshape(
            1, vertical_extent * streamwise_extent
        )
        arrhenius = arrhenius_prefactor[:, None] * jnp.exp(
            -ignition_energy_ratio[:, None] / enthalpy_output
        )
        reacted = react(
            block, arrhenius, left_bilinear_weights, right_bilinear_weights, species_yield_weights
        )
        reacted = reacted.reshape(species_count, 1, vertical_extent, streamwise_extent)
        return lax.dynamic_update_slice_in_dim(current, reacted, starting_ensemble, 1)

    return lax.fori_loop(0, planes, one_plane, carried_ensemble)


def body(
    composition_vector,
    filtered_motion,
    spreading_strength,
    blend_relax_multiplier,
    thermal_level,
    brownian_jumps,
    left_bilinear_weights,
    right_bilinear_weights,
    species_yield_weights,
    arrhenius_prefactor,
    ignition_energy_ratio,
):
    fields = lax.axis_size("field")
    motion_lookup, spreading_gradient_sum, subgrid_blend_sum, thermal_lookup = (
        lax.all_gather(filtered_motion, "field", axis=2, tiled=True),
        lax.all_gather(spreading_strength, "field", axis=1, tiled=True),
        lax.all_gather(blend_relax_multiplier, "field", axis=1, tiled=True),
        lax.all_gather(thermal_level, "field", axis=1, tiled=True),
    )
    current = composition_vector[0]
    for step in range(STEPS):
        mean = lax.psum(current, "field") / fields
        padded = extended(current, (("space", 1),), 1)
        carried_ensemble = transport(
            padded,
            current,
            mean,
            motion_lookup,
            spreading_gradient_sum,
            subgrid_blend_sum,
            brownian_jumps[step, 0],
        )
        current = kinetic_yield_term(
            carried_ensemble,
            thermal_lookup,
            arrhenius_prefactor,
            ignition_energy_ratio,
            left_bilinear_weights,
            right_bilinear_weights,
            species_yield_weights,
        )
    return current[None]


def solution(mesh):
    return jax.shard_map(
        body,
        mesh=mesh,
        in_specs=(
            P("field", None, "space", None, None),
            P(None, "space", "field", None),
            P("space", "field", None),
            P("space", "field", None),
            P("space", "field", None),
            P(None, "field", None),
            P(),
            P(),
            P(),
            P(),
            P(),
        ),
        out_specs=P("field", None, "space", None, None),
        check_vma=False,
    )
```

profile of v0, /device:TPU:0, one launch (start us, length us, event | category | flops | bytes accessed | tf_op | source)
XLA Modules:
  0.0 189.9 jit_solution(7021989027191546561)
XLA Ops:
  6.5 1.3 copy.61
  7.9 6.1 %collective-permute-start = (f32[32,1,16,128]{3,2,0,1:T(8,128)S(1)}, f32[32,1,16,128]{3,2,0,1:T(8,128)S(1)}, u32[]{:S(2)}, u32[]{:S(2)}) collective-permute-start(f32[32,1,16,128]{3,2,0,1:T(8,128)S(1)} %get-tuple-element.464), channel_id=1, source_target_pairs={{4,0},{8,4},{12,8},{16,12},{20,16},{24,20},{28,24},{0,28},{5,1},{9... | collective-permute-start | bytes 786440 | tf_op jit(solution)/shard_map/ppermute | solution.py:21
  14.1 3.1 %fusion.87 = (f32[32,4,15,128]{3,2,0,1:T(8,128)}, f32[32,4,15,128]{3,2,0,1:T(8,128)}) fusion(f32[32,4,16,128]{3,2,0,1:T(8,128)} %bitcast.365), kind=kLoop, calls=%fused_computation.139 | loop fusion | bytes 3932160 | tf_op jit(solution)/shard_map/jit(_roll_static)/slice | solution.py:29
  17.2 1.6 fusion.89
  18.9 1.7 fusion.90
  20.6 6.0 %all_gather.12 = f32[3,4,16,128]{3,1,0,2:T(4,128)S(1)} all-gather(f32[3,4,4,128]{3,1,0,2:T(4,128)S(1)} %copy.29), channel_id=1, replica_groups=mesh['space'=8,'field'=4] {'field'}, dimensions={2}, use_global_device_ids=true | all-gather | bytes 122880 | tf_op jit(solution)/shard_map/all_gather | solution.py:103
  29.2 5.2 %all_gather.13 = f32[4,16,128]{2,0,1:T(4,128)S(1)} all-gather(f32[4,4,128]{2,0,1:T(4,128)S(1)} %copy.33), channel_id=1, replica_groups=mesh['space'=8,'field'=4] {'field'}, dimensions={1}, use_global_device_ids=true | all-gather | bytes 40960 | tf_op jit(solution)/shard_map/all_gather | solution.py:104
  34.4 5.2 %all_gather.14 = f32[4,16,128]{2,0,1:T(4,128)S(1)} all-gather(f32[4,4,128]{2,0,1:T(4,128)S(1)} %copy.36), channel_id=1, replica_groups=mesh['space'=8,'field'=4] {'field'}, dimensions={1}, use_global_device_ids=true | all-gather | bytes 40960 | tf_op jit(solution)/shard_map/all_gather | solution.py:105
  39.6 5.2 %all_gather.15 = f32[4,16,128]{2,0,1:T(4,128)S(1)} all-gather(f32[4,4,128]{2,0,1:T(4,128)S(1)} %copy.38), channel_id=1, replica_groups=mesh['space'=8,'field'=4] {'field'}, dimensions={1}, use_global_device_ids=true | all-gather | bytes 40960 | tf_op jit(solution)/shard_map/all_gather | solution.py:106
  46.8 5.6 %all-reduce.3.cloned.1.call-done = f32[32,4,16,128]{3,2,0,1:T(8,128)} async-done(((f32[32,4,16,128]{3,2,0,1:T(8,128)}), f32[32,4,16,128]{3,2,0,1:T(8,128)}) %all-reduce.3.cloned.1.call-update) | async-done | bytes 1048592 | tf_op jit(solution)/shard_map/psum | solution.py:110
  52.5 3.9 %multiply_subtract_fusion.1 = f32[32,4,16,128]{3,2,0,1:T(8,128)S(1)} fusion(f32[32,4,16,128]{3,2,0,1:T(8,128)S(1)} %bitcast.369, f32[32,4,16,128]{3,2,0,1:T(8,128)} %all-reduce.3.cloned.1.call-done, f32[32,4,16,127]{3,2,0,1:T(8,128)} %get-tuple-element.470, f32[32,4,16,1]{3,2,0,1:T(8,128)} %get-tuple-element.472, f32[32,4,16,1]{3,2,0,1:T(8,128)} %get-tuple-element.471, ...), kind=kLoop, calls=%fused_computation.125 | loop fusion | flops 9175040 | bytes 8060940 | tf_op jit(solution)/shard_map/sub | solution.py:41
  56.4 43.6 %while.30 = (s32[]{:T(128)}, f32[32,4,16,128]{3,2,0,1:T(8,128)S(1)}, f32[206]{0:T(256)S(1)}, f32[206,1]{0,1:T(1,128)S(1)}, f32[4,16,128]{2,1,0:T(8,128)S(1)}, /*...) while((s32[]{:T(128)}, ...), condition=%wide.region_2.3_spmd, body=%wide.region_1.2_spmd.sunk | while | flops 427352064 | bytes 22643992 | solution.py:85
  56.9 1.7 fusion.202
  59.1 1.7 fusion.203
  61.2 1.7 fusion.204
  63.4 1.7 fusion.205
  65.5 1.7 fusion.206
  67.8 1.7 fusion.202
  70.0 1.7 fusion.203
  72.1 1.7 fusion.204
  74.3 1.7 fusion.205
  76.4 1.7 fusion.206
  78.7 1.7 fusion.202
  80.9 1.7 fusion.203
  83.0 1.7 fusion.204
  85.2 1.7 fusion.205
  87.3 1.7 fusion.206
  89.6 1.7 fusion.202
  91.8 1.7 fusion.203
  93.9 1.7 fusion.204
  96.1 1.7 fusion.205
  98.2 1.7 fusion.206
  100.1 1.3 fusion.82
  101.4 1.6 fusion.84
  103.8 4.5 %collective-permute-start.2 = (f32[32,1,16,128]{3,2,0,1:T(8,128)}, f32[32,1,16,128]{3,2,0,1:T(8,128)S(1)}, u32[]{:S(2)}, u32[]{:S(2)}) collective-permute-start(f32[32,1,16,128]{3,2,0,1:T(8,128)} %get-tuple-element.454), channel_id=1, source_target_pairs={{4,0},{8,4},{12,8},{16,12},{20,16},{24,20},{28,24},{0,28},{5,1},{9... | collective-permute-start | bytes 786440 | tf_op jit(solution)/shard_map/ppermute | solution.py:21
  108.2 1.7 fusion.85
  110.0 3.3 %collective-permute-done.2 = f32[32,1,16,128]{3,2,0,1:T(8,128)S(1)} collective-permute-done((f32[32,1,16,128]{3,2,0,1:T(8,128)}, f32[32,1,16,128]{3,2,0,1:T(8,128)S(1)}, u32[]{:S(2)}, u32[]{:S(2)}) %collective-permute-start.2) | collective-permute-done | bytes 262176 | tf_op jit(solution)/shard_map/ppermute | solution.py:21
  113.3 4.6 %collective-permute-done.3 = f32[32,1,16,128]{3,2,0,1:T(8,128)S(1)} collective-permute-done((f32[32,1,16,128]{3,2,0,1:T(8,128)S(1)}, f32[32,1,16,128]{3,2,0,1:T(8,128)S(1)}, u32[]{:S(2)}, u32[]{:S(2)}) %collective-permute-start.3) | collective-permute-done | bytes 262176 | tf_op jit(solution)/shard_map/ppermute | solution.py:20
  117.9 22.7 %all-reduce.5.cloned.1.call-done = f32[32,4,16,128]{3,2,0,1:T(8,128)} async-done(((f32[32,4,16,128]{3,2,0,1:T(8,128)}), f32[32,4,16,128]{3,2,0,1:T(8,128)}) %all-reduce.5.cloned.1.call-update) | async-done | bytes 1048592 | tf_op jit(solution)/shard_map/psum | solution.py:110
  140.6 4.4 %multiply_subtract_fusion = f32[32,4,16,128]{3,2,0,1:T(8,128)} fusion(f32[32,4,16,128]{3,2,0,1:T(8,128)S(1)} %copy-done.1, f32[32,4,16,128]{3,2,0,1:T(8,128)} %all-reduce.5.cloned.1.call-done, f32[32,4,16,127]{3,2,0,1:T(8,128)} %get-tuple-element.460, f32[32,4,16,1]{3,2,0,1:T(8,128)} %get-tuple-element.462, f32[32,4,16,1]{3,2,0,1:T(8,128)} %get-tuple-element.461, ...), kind=kLoop, calls=%fused_computation.124 | loop fusion | flops 9175040 | bytes 8060940 | tf_op jit(solution)/shard_map/sub | solution.py:41
  145.0 35.8 %while.31 = (s32[]{:T(128)}, f32[32,4,16,128]{3,2,0,1:T(8,128)}, f32[206]{0:T(256)S(1)}, f32[206,1]{0,1:T(1,128)S(1)}, f32[4,16,128]{2,1,0:T(8,128)S(1)}, /*inde...) while((s32[]{:T(128)}, f32[32,4,16,128]{3,2,0,1:T(8,128)}, ...), condition=%wide.region_5.6_spmd, body=%wide.region_4.5_spmd.sunk | while | flops 427352064 | bytes 22644500 | solution.py:85
  146.4 1.0 fusion.230
  155.3 1.0 fusion.230
  156.8 1.0 fusion.231
  158.2 1.0 fusion.232
  164.3 1.0 fusion.230
  173.2 1.0 fusion.230
  180.7 2.3 %copy.60 = f32[32,4,16,128]{3,2,1,0:T(8,128)} copy(f32[32,4,16,128]{3,2,0,1:T(8,128)} %get-tuple-element.388) | data formatting | bytes 2097152 | tf_op jit(solution)/shard_map/while | solution.py:85
  (139 shorter events, 39.9 us)
Async XLA Ops:
  6.5 45.9 %all-reduce.3.cloned.1.call-start = ((), (), s32[]{:S(2)}) async-start(), calls=%async_computation | async-start | bytes 2097152 | tf_op jit(solution)/shard_map/psum | solution.py:110
  7.9 6.1 %copy-start.2 = (f32[1,32,4,16,128]{4,3,1,2,0:T(8,128)}, f32[1,32,4,16,128]{4,3,1,2,0:T(8,128)S(1)}, u32[]{:S(2)}) copy-start(f32[1,32,4,16,128]{4,3,1,2,0:T(8,128)S(1)} %copy.61) | copy-start | bytes 3145732
  7.9 38.9 %collective-permute-start = (f32[32,1,16,128]{3,2,0,1:T(8,128)S(1)}, f32[32,1,16,128]{3,2,0,1:T(8,128)S(1)}, u32[]{:S(2)}, u32[]{:S(2)}) collective-permute-start(f32[32,1,16,128]{3,2,0,1:T(8,128)S(1)} %get-tuple-element.464), channel_id=1, source_target_pairs={{4,0},{8,4},{12,8},{16,12},{20,16},{24,20},{28,24},{0,28},{5,1},{9... | collective-permute-start | bytes 786440 | tf_op jit(solution)/shard_map/ppermute | solution.py:21
  14.0 32.9 %collective-permute-start.1 = (f32[32,1,16,128]{3,2,0,1:T(8,128)S(1)}, f32[32,1,16,128]{3,2,0,1:T(8,128)S(1)}, u32[]{:S(2)}, u32[]{:S(2)}) collective-permute-start(f32[32,1,16,128]{3,2,0,1:T(8,128)S(1)} %get-tuple-element.463), channel_id=1, source_target_pairs={{0,4},{4,8},{8,12},{12,16},{16,20},{20,24},{24,28},{28,0},{1,5},{5... | collective-permute-start | bytes 786440 | tf_op jit(solution)/shard_map/ppermute | solution.py:20
  14.0 3.2 %copy-start.3 = (f32[1,32,4,16,128]{4,3,1,2,0:T(8,128)S(1)}, f32[1,32,4,16,128]{4,3,1,2,0:T(8,128)}, u32[]{:S(2)}) copy-start(f32[1,32,4,16,128]{4,3,1,2,0:T(8,128)} %copy-done.2) | copy-start | bytes 3145732
  14.0 126.6 %all-reduce.5.cloned.1.call-start = ((), (), s32[]{:S(2)}) async-start(), calls=%async_computation.1 | async-start | bytes 2097152 | tf_op jit(solution)/shard_map/psum | solution.py:110
  18.8 1.7 copy-start.5
  18.8 7.7 %copy-start.6 = (f32[2,1,3]{2,1,0:T(1,128)S(1)}, f32[2,1,3]{2,1,0:T(1,128)}, u32[]{:S(2)}) copy-start(f32[2,1,3]{2,1,0:T(1,128)} %param.20) | copy-start | bytes 76
  18.8 10.3 %copy-start.7 = (f32[4,4,128]{2,1,0:T(4,128)S(1)}, f32[4,4,128]{2,1,0:T(4,128)}, u32[]{:S(2)}) copy-start(f32[4,4,128]{2,1,0:T(4,128)} %param.17) | copy-start | bytes 24580
  18.8 10.3 %copy-start.8 = (f32[4,4,128]{2,1,0:T(4,128)S(1)}, f32[4,4,128]{2,1,0:T(4,128)}, u32[]{:S(2)}) copy-start(f32[4,4,128]{2,1,0:T(4,128)} %param.18) | copy-start | bytes 24580
  18.8 20.7 %copy-start.9 = (f32[4,4,128]{2,1,0:T(4,128)S(1)}, f32[4,4,128]{2,1,0:T(4,128)}, u32[]{:S(2)}) copy-start(f32[4,4,128]{2,1,0:T(4,128)} %param.19) | copy-start | bytes 24580
  18.9 25.9 %copy-start.10 = (f32[206]{0:T(256)S(1)}, f32[206]{0:T(256)}, u32[]{:S(2)}) copy-start(f32[206]{0:T(256)} %param.25) | copy-start | bytes 2476
  52.5 3.9 %copy-start.4 = (bf16[206,32]{0,1:T(8,128)(2,1)S(1)}, bf16[206,32]{0,1:T(8,128)(2,1)}, u32[]{:S(2)}) copy-start(bf16[206,32]{0,1:T(8,128)(2,1)} %param.21) | copy-start | bytes 39556
  52.5 4.0 %copy-start.11 = (bf16[206,32]{0,1:T(8,128)(2,1)S(1)}, bf16[206,32]{0,1:T(8,128)(2,1)}, u32[]{:S(2)}) copy-start(bf16[206,32]{0,1:T(8,128)(2,1)} %param.22) | copy-start | bytes 39556
  52.5 4.0 %copy-start.13 = (f32[206]{0:T(256)S(1)}, f32[206]{0:T(256)}, u32[]{:S(2)}) copy-start(f32[206]{0:T(256)} %param.24) | copy-start | bytes 2476
  100.1 3.0 %copy-start = (f32[32,4,16,128]{3,2,0,1:T(8,128)}, f32[32,4,16,128]{3,2,0,1:T(8,128)S(1)}, u32[]{:S(2)}) copy-start(f32[32,4,16,128]{3,2,0,1:T(8,128)S(1)} %get-tuple-element.387) | copy-start | bytes 3145732
  103.8 4.5 %copy-start.1 = (f32[32,4,16,128]{3,2,0,1:T(8,128)S(1)}, f32[32,4,16,128]{3,2,0,1:T(8,128)}, u32[]{:S(2)}) copy-start(f32[32,4,16,128]{3,2,0,1:T(8,128)} %copy-done) | copy-start | bytes 3145732
  103.8 9.6 %collective-permute-start.2 = (f32[32,1,16,128]{3,2,0,1:T(8,128)}, f32[32,1,16,128]{3,2,0,1:T(8,128)S(1)}, u32[]{:S(2)}, u32[]{:S(2)}) collective-permute-start(f32[32,1,16,128]{3,2,0,1:T(8,128)} %get-tuple-element.454), channel_id=1, source_target_pairs={{4,0},{8,4},{12,8},{16,12},{20,16},{24,20},{28,24},{0,28},{5,1},{9... | collective-permute-start | bytes 786440 | tf_op jit(solution)/shard_map/ppermute | solution.py:21
  108.2 9.7 %collective-permute-start.3 = (f32[32,1,16,128]{3,2,0,1:T(8,128)S(1)}, f32[32,1,16,128]{3,2,0,1:T(8,128)S(1)}, u32[]{:S(2)}, u32[]{:S(2)}) collective-permute-start(f32[32,1,16,128]{3,2,0,1:T(8,128)S(1)} %get-tuple-element.453), channel_id=1, source_target_pairs={{0,4},{4,8},{8,12},{12,16},{16,20},{20,24},{24,28},{28,0},{1,5},{5... | collective-permute-start | bytes 786440 | tf_op jit(solution)/shard_map/ppermute | solution.py:20
  140.6 4.4 %copy-start.12 = (bf16[32,206]{1,0:T(8,128)(2,1)S(1)}, bf16[32,206]{1,0:T(8,128)(2,1)}, u32[]{:S(2)}) copy-start(bf16[32,206]{1,0:T(8,128)(2,1)} %get-tuple-element.655) | copy-start | bytes 39556
Sparse Core Ops, SparseCore 0:
  14.1 38.2 all-reduce.2
  103.9 36.6 all-reduce.4
where the time goes:
time: 192 us; the launch traced here: 190 us
  matrix products  71.1 us (37%)
  waiting for transfers between devices  36.2 us (19%)
  local copies, waits for them, and re-layouts  23.9 us (12%)
  blocking collectives  21.5 us (11%)
  between operations  17.4 us (9%)
  starting transfers between devices  10.6 us (6%)
  other arithmetic  8.37 us (4%)
    dot_general x40, matrix products, react(): jnp.dot(species_yield_weights, rates, preferred_element_type=jnp.float32)  54.5 us
    psum x2, waiting for transfers between devices, body(): mean = lax.psum(current, 'field') / fields  28.3 us
    dot_general x40, matrix products, react(): jnp.dot(left_bilinear_weights, lowered, preferred_element_type=jnp.float32)  16.6 us
    ppermute x2, starting transfers between devices, extended(): after = lax.ppermute(leading, axis, down)  10.5 us
    sub x2, other arithmetic, transport(): current - advect + spreading_strength * laplace + noise  8.33 us
    slice x4, local copies, waits for them, and re-layouts, transport(): z_plus = jnp.roll(current, -1, 3)  6.63 us
    all_gather x1, blocking collectives, body(): lax.all_gather(filtered_motion, 'field', axis=2, tiled=True)  5.96 us
    all_gather x1, blocking collectives, body(): lax.all_gather(thermal_level, 'field', axis=1, tiled=True)  5.19 us
  transfers between devices with their start and end apart: 6, of which 4 were waited for; matrix products, arithmetic and copies ran while one was open for 5% of the time, Pallas kernels for 0%

commit v1 on v0

v1 whole, which is shorter than its diff:
```python
import functools

import jax
import jax.numpy as jnp
from jax import lax
from jax.experimental import pallas as pl
from jax.experimental.pallas import tpu as pltpu
from jax.sharding import PartitionSpec as P

STEPS = 2
SUB = 5
TILE_ROWS = 8

chem_step = 0.2

MESH = pl.DeviceIdType.MESH


def kernel(
    fields,
    spaces,
    wiener,
    inp,
    motion,
    spread,
    blend,
    thermal,
    left_w,
    right_w,
    yield_w,
    prefactor,
    ignition,
    out,
    current1,
    partner_planes,
    chip_half,
    other_sums,
    halo,
    motion_g,
    spread_g,
    blend_g,
    thermal_g,
    arrhenius,
    left_p,
    right_p,
    yield_p,
    column,
    pre_b,
    ign_b,
    flow_send,
    flow_recv,
    pair_send,
    pair_recv,
    cross_send,
    cross_recv,
    relay_send,
    relay_recv,
    halo_send,
    halo_recv,
):
    planes, rows, species, lanes = inp.shape
    reactions = left_w.shape[0]
    padded = left_p.shape[0]
    half = rows // 2
    chips = fields // 2
    local_rows = spread.shape[1]
    me = lax.axis_index("field")
    slab = lax.axis_index("space")
    core = lax.rem(me, 2)
    chip = lax.div(me, 2)
    partner = chip * 2 + 1 - core
    right = lax.rem(slab + 1, spaces)
    left = lax.rem(slab + spaces - 1, spaces)
    mine = pl.ds(core * half, half)
    others = pl.ds((1 - core) * half, half)
    order = list(range(1, planes - 1)) + [0, planes - 1]

    barrier = pltpu.get_barrier_semaphore()
    for d in range(1, fields):
        pl.semaphore_signal(
            barrier, inc=1, device_id={"field": lax.rem(me + d, fields)}, device_id_type=MESH
        )
    for neighbour in (left, right):
        pl.semaphore_signal(barrier, inc=1, device_id={"space": neighbour}, device_id_type=MESH)
    pl.semaphore_wait(barrier, fields + 1)

    def remote(src, dst, send, recv, **to):
        return pltpu.make_async_remote_copy(
            src_ref=src,
            dst_ref=dst,
            send_sem=send,
            recv_sem=recv,
            device_id=to,
            device_id_type=MESH,
        )

    sources = [inp, current1]

    def pair_copy(step, p):
        return remote(
            sources[step].at[p],
            partner_planes.at[step, p],
            pair_send.at[step, p],
            pair_recv.at[step, p],
            field=partner,
        )

    def cross_copy(step, p, d):
        return remote(
            chip_half.at[step, p],
            other_sums.at[step, p, d - 1, mine],
            cross_send.at[step, p, d - 1],
            cross_recv.at[step, p, d - 1],
            field=lax.rem(chip + d, chips) * 2 + core,
        )

    def relay_copy(step, p, d):
        return remote(
            other_sums.at[step, p, d - 1, mine],
            other_sums.at[step, p, d - 1, mine],
            relay_send.at[step, p, d - 1],
            relay_recv.at[step, p, d - 1],
            field=partner,
        )

    def halo_copy(step, side):
        return remote(
            sources[step].at[planes - 1 if side == 0 else 0],
            halo.at[step, side],
            halo_send.at[step, side],
            halo_recv.at[step, side],
            space=right if side == 0 else left,
        )

    flow_pairs = [(thermal, thermal_g), (motion, motion_g), (spread, spread_g), (blend, blend_g)]

    def flow_copy(k, d):
        src, dst = flow_pairs[k]
        return remote(
            src,
            dst.at[me],
            flow_send.at[k, d - 1],
            flow_recv.at[k, d - 1],
            field=lax.rem(me + d, fields),
        )

    pair_copy(0, order[0]).start()
    for k in range(4):
        for d in range(1, fields):
            flow_copy(k, d).start()
    for p in order[1:]:
        pair_copy(0, p).start()
    for side in range(2):
        halo_copy(0, side).start()
    for src, dst in flow_pairs:
        dst[me] = src[...]

    left_p[...] = jnp.zeros_like(left_p)
    right_p[...] = jnp.zeros_like(right_p)
    yield_p[...] = jnp.zeros_like(yield_p)
    left_p[0:reactions, :] = left_w[...]
    right_p[0:reactions, :] = right_w[...]
    yield_p[:, 0:reactions] = yield_w[...]
    for src, dst in ((prefactor, pre_b), (ignition, ign_b)):
        column[...] = jnp.zeros_like(column)
        column[0:1, 0:reactions] = src[...]
        spread_rows = jnp.broadcast_to(column[0:1, :], (lanes, column.shape[1]))
        dst[...] = jnp.transpose(spread_rows)[0:padded, :]

    def reduce_pair(step, p):
        pair_copy(step, p).wait_recv()
        chip_half[step, p] = sources[step][p, mine] + partner_planes[step, p, mine]

    def send_cross(step, p):
        for d in range(1, chips):
            cross_copy(step, p, d).start()

    def relay(step, p):
        for d in range(1, chips):
            cross_copy(step, p, d).wait_recv()
            relay_copy(step, p, d).start()

    for i, p in enumerate(order):
        reduce_pair(0, p)
        if i > 0:
            send_cross(0, order[i - 1])
    for k in range(4):
        for d in range(1, fields):
            flow_copy(k, d).wait_recv()
    send_cross(0, order[-1])

    def arrhenius_rows(p):
        def one(g, carry):
            for r in range(local_rows):
                inverse = 1.0 / thermal_g[g, p, r : r + 1, :]
                arrhenius[p * rows + g * local_rows + r] = pre_b[...] * jnp.exp(
                    -(ign_b[...] * jnp.broadcast_to(inverse, (padded, lanes)))
                )
            return carry

        lax.fori_loop(0, fields, one, 0)

    def transport(step, p, dst):
        src = sources[step]
        before = halo.at[step, 0] if p == 0 else src.at[p - 1]
        after = halo.at[step, 1] if p == planes - 1 else src.at[p + 1]
        w = [wiener[step, 0, k] for k in range(3)]

        def one(g, carry):
            for r in range(local_rows):
                y = g * local_rows + r
                d_row = spread_g[g, p, r : r + 1, :]
                mix = blend_g[g, p, r : r + 1, :]
                noise = jnp.sqrt(2.0 * d_row)
                e = [0.5 * (motion_g[g, k, p, r : r + 1, :] - noise * w[k]) for k in range(3)]
                centre = 1.0 - 6.0 * d_row - mix
                own = src[p, y]
                y_up = src[p, lax.rem(y + 1, rows)]
                y_down = src[p, lax.rem(y + rows - 1, rows)]
                total = own + partner_planes[step, p, y]
                for d in range(1, chips):
                    total = total + other_sums[step, p, d - 1, y]
                moved = centre * own + (mix * (1.0 / fields)) * total
                moved = moved + (d_row - e[0]) * after[y] + (d_row + e[0]) * before[y]
                moved = moved + (d_row - e[1]) * y_up + (d_row + e[1]) * y_down
                moved = moved + (d_row - e[2]) * pltpu.roll(own, lanes - 1, 1)
                moved = moved + (d_row + e[2]) * pltpu.roll(own, 1, 1)
                dst[p, y] = moved
            return carry

        lax.fori_loop(0, fields, one, 0)

    def chemistry(p, first, last, dst):
        def one(substep, carry):
            for base in range(0, rows, TILE_ROWS):
                block = jnp.concatenate([dst[p, base + i] for i in range(TILE_ROWS)], axis=1)
                low = block.astype(jnp.bfloat16)
                forward = jnp.dot(left_p[...], low, preferred_element_type=jnp.float32)
                backward = jnp.dot(right_p[...], low, preferred_element_type=jnp.float32)
                level = jnp.concatenate(
                    [arrhenius[p * rows + base + i] for i in range(TILE_ROWS)], axis=1
                )
                saturation = 1.0 + forward * forward + backward * backward
                rates = (level * forward * backward / saturation).astype(jnp.bfloat16)
                block = block + chem_step * jnp.dot(
                    yield_p[:, 0:padded], rates, preferred_element_type=jnp.float32
                )
                for i in range(TILE_ROWS):
                    dst[p, base + i] = block[:, i * lanes : (i + 1) * lanes]
            return carry

        lax.fori_loop(first, last, one, 0)

    for p in order[:1]:
        arrhenius_rows(p)
    relay(0, order[0])
    for p in order[1:]:
        arrhenius_rows(p)

    middle = SUB // 2
    for k in range(STEPS * planes):
        step, i = divmod(k, planes)
        p = order[i]
        dst = current1 if step < STEPS - 1 else out
        for d in range(1, chips):
            relay_copy(step, p, d).wait_recv()
        if p == 0:
            halo_copy(step, 0).wait_recv()
        if p == planes - 1:
            halo_copy(step, 1).wait_recv()
        transport(step, p, dst)
        chemistry(p, 0, middle, dst)
        if k < planes - 1:
            relay(0, order[k + 1])
        if 2 <= k < planes + 2:
            relay(1, order[k - 2])
        if 1 <= k < planes + 1:
            reduce_pair(1, order[k - 1])
        chemistry(p, middle, SUB, dst)
        if 1 <= k < planes + 1:
            send_cross(1, order[k - 1])
        if step == 0:
            pair_copy(1, p).start()
            if p == planes - 1:
                halo_copy(1, 0).start()
            if p == 0:
                halo_copy(1, 1).start()

    for step in range(STEPS):
        for p in range(planes):
            pair_copy(step, p).wait_send()
            for d in range(1, chips):
                cross_copy(step, p, d).wait_send()
                relay_copy(step, p, d).wait_send()
        for side in range(2):
            halo_copy(step, side).wait_send()
    for k in range(4):
        for d in range(1, fields):
            flow_copy(k, d).wait_send()


def body(
    fields,
    spaces,
    composition_vector,
    filtered_motion,
    spreading_strength,
    blend_relax_multiplier,
    thermal_level,
    brownian_jumps,
    left_bilinear_weights,
    right_bilinear_weights,
    species_yield_weights,
    arrhenius_prefactor,
    ignition_energy_ratio,
):
    _, species, planes, rows, lanes = composition_vector.shape
    reactions = left_bilinear_weights.shape[0]
    padded = -(-reactions // 16) * 16
    wide = -(-padded // 128) * 128
    local_rows = spreading_strength.shape[1]
    chips = fields // 2
    others = max(chips - 1, 1)
    f32 = jnp.float32
    vmem = pl.BlockSpec(memory_space=pltpu.VMEM)
    state = jnp.transpose(composition_vector[0], (1, 2, 0, 3))
    result = pl.pallas_call(
        functools.partial(kernel, fields, spaces),
        out_shape=jax.ShapeDtypeStruct(state.shape, f32),
        in_specs=[pl.BlockSpec(memory_space=pltpu.SMEM)] + [vmem] * 10,
        out_specs=vmem,
        scratch_shapes=[
            pltpu.VMEM((planes, rows, species, lanes), f32),
            pltpu.VMEM((STEPS, planes, rows, species, lanes), f32),
            pltpu.VMEM((STEPS, planes, rows // 2, species, lanes), f32),
            pltpu.VMEM((STEPS, planes, others, rows, species, lanes), f32),
            pltpu.VMEM((STEPS, 2, rows, species, lanes), f32),
            pltpu.VMEM((fields, 3, planes, local_rows, lanes), f32),
            pltpu.VMEM((fields, planes, local_rows, lanes), f32),
            pltpu.VMEM((fields, planes, local_rows, lanes), f32),
            pltpu.VMEM((fields, planes, local_rows, lanes), f32),
            pltpu.VMEM((planes * rows, padded, lanes), f32),
            pltpu.VMEM((padded, species), jnp.bfloat16),
            pltpu.VMEM((padded, species), jnp.bfloat16),
            pltpu.VMEM((species, wide), jnp.bfloat16),
            pltpu.VMEM((8, wide), f32),
            pltpu.VMEM((padded, lanes), f32),
            pltpu.VMEM((padded, lanes), f32),
            pltpu.SemaphoreType.DMA((4, fields)),
            pltpu.SemaphoreType.DMA((4, fields)),
            pltpu.SemaphoreType.DMA((STEPS, planes)),
            pltpu.SemaphoreType.DMA((STEPS, planes)),
            pltpu.SemaphoreType.DMA((STEPS, planes, others)),
            pltpu.SemaphoreType.DMA((STEPS, planes, others)),
            pltpu.SemaphoreType.DMA((STEPS, planes, others)),
            pltpu.SemaphoreType.DMA((STEPS, planes, others)),
            pltpu.SemaphoreType.DMA((STEPS, 2)),
            pltpu.SemaphoreType.DMA((STEPS, 2)),
        ],
        compiler_params=pltpu.CompilerParams(
            collective_id=0, has_side_effects=True, vmem_limit_bytes=60 * 1024 * 1024
        ),
        name="fields_step",
    )(
        brownian_jumps,
        state,
        filtered_motion,
        spreading_strength,
        blend_relax_multiplier,
        thermal_level,
        left_bilinear_weights,
        right_bilinear_weights,
        species_yield_weights,
        arrhenius_prefactor[None],
        ignition_energy_ratio[None],
    )
    return jnp.transpose(result, (2, 0, 1, 3))[None]


def solution(mesh):
    return jax.shard_map(
        functools.partial(body, mesh.shape["field"], mesh.shape["space"]),
        mesh=mesh,
        in_specs=(
            P("field", None, "space", None, None),
            P(None, "space", "field", None),
            P("space", "field", None),
            P("space", "field", None),
            P("space", "field", None),
            P(None, "field", None),
            P(),
            P(),
            P(),
            P(),
            P(),
        ),
        out_specs=P("field", None, "space", None, None),
        check_vma=False,
    )
```

time: 192 us -> 78.6 us (0.41)
  matrix products: 71.1 us -> 0 us
  Pallas kernels: 0 us -> 70.5 us
  waiting for transfers between devices: 36.2 us -> 0 us
  blocking collectives: 21.5 us -> 0 us
  between operations: 17.4 us -> 0.01 us
  local copies, waits for them, and re-layouts: 23.9 us -> 7.77 us
  starting transfers between devices: 10.6 us -> 0 us
  other arithmetic: 8.37 us -> 0 us
    dot_general x80 -> x0, matrix products: 71.1 us -> none  [the longest x40 54.5 us: react(): jnp.dot(species_yield_weights, rates, preferred_element_type=jnp.float32)]
    pallas_call x0 -> x1, Pallas kernels: none -> 70.5 us  [body(): pl.pallas_call(functools.partial(kernel, fields, spaces), out_shape=jax.S...]
    psum x2 -> x0, waiting for transfers between devices: 28.3 us -> none  [body(): mean = lax.psum(current, 'field') / fields]
    all_gather x4 -> x0, blocking collectives: 21.5 us -> none  [the longest x1 5.96 us: body(): lax.all_gather(filtered_motion, 'field', axis=2, tiled=True)]
    slice x11 -> x0, local copies, waits for them, and re-layouts: 12.7 us -> none  [the longest x4 6.63 us: transport(): z_plus = jnp.roll(current, -1, 3)]
    ppermute x4 -> x0, starting transfers between devices: 10.5 us -> none  [the longest x2 10.5 us: extended(): after = lax.ppermute(leading, axis, down)]
    sub x2 -> x0, other arithmetic: 8.33 us -> none  [transport(): current - advect + spreading_strength * laplace + noise]
    ppermute x4 -> x0, waiting for transfers between devices: 7.92 us -> none  [the longest x2 4.59 us: extended(): before = lax.ppermute(last, axis, up)]
  transfers between devices with their start and end apart: 6 -> 0, of which waited for: 4 -> 0; matrix products, arithmetic and copies ran while one was open for 5% -> 0% of each run, Pallas kernels for 0% -> 0%
where the time goes in v1:
time: 78.6 us; the launch traced here: 78.3 us
  Pallas kernels  70.5 us (90%)
  local copies, waits for them, and re-layouts  7.77 us (10%)
    pallas_call x1, Pallas kernels, body(): pl.pallas_call(functools.partial(kernel, fields, spaces), out_shape=jax.S...  70.5 us
    unnamed x5, local copies, waits for them, and re-layouts  4.96 us
    broadcast_in_dim x1, local copies, waits for them, and re-layouts, body(): return jnp.transpose(result, (2, 0, 1, 3))[None]  2.81 us

profile of v1, /device:TPU:0, one launch (start us, length us, event | category | flops | bytes accessed | tf_op | source)
XLA Modules:
  0.0 78.3 jit_solution(8301183912856756931)
XLA Ops:
  0.0 0.0 copy-start
  0.0 1.4 %copy.13.left_w = bf16[206,32]{1,0:T(8,128)(2,1)} copy(bf16[206,32]{0,1:T(8,128)(2,1)} %param.17) | data formatting | bytes 26368 | tf_op args[6]
  1.4 0.0 copy-done
  1.5 0.7 copy.14.right_w
  2.2 2.8 %copy.17 = f32[1,32,4,16,128]{4,1,3,2,0:T(8,128)} copy(f32[1,32,4,16,128]{4,3,2,1,0:T(8,128)} %param.11) | data formatting | bytes 2097152 | tf_op args[0]
  5.0 70.5 %fields_step.1 = f32[4,16,32,128]{3,2,1,0:T(8,128)} custom-call(f32[2,1,3]{2,1,0:T(1,128)} %wiener.1, f32[4,16,32,128]{3,2,1,0:T(8,128)} %bitcast.11, f32[3,4,4,128]{3,2,1,0:T(4,128)} %motion.1, f32[4,4,128]{2,1,0:T(4,128)} %spread.1, f32[4,4,128]{2,1,0:T(4,128)} %blend.1, f32[4,4,128]{2,1,0:T(4,128)} %thermal.1, bf16[206,32]{1,0:T(8,128)(2,1)} %copy.13.left_w, ...), custom_call_target="tpu_custom_call" | custom-call | tf_op jit(solution)/shard_map/fields_step/pallas_call | solution.py:327
  75.5 2.8 %copy.15 = f32[1,32,4,16,128]{4,3,2,1,0:T(8,128)} copy(f32[1,32,4,16,128]{4,1,3,2,0:T(8,128)} %bitcast.10) | data formatting | bytes 2097152 | tf_op jit(solution)/shard_map/broadcast_in_dim | solution.py:377
Async XLA Ops:
  0.0 1.5 %copy-start = (bf16[206,32]{0,1:T(8,128)(2,1)S(1)}, bf16[206,32]{0,1:T(8,128)(2,1)}, u32[]{:S(2)}) copy-start(bf16[206,32]{0,1:T(8,128)(2,1)} %param.18) | copy-start | bytes 39556

commit v2 on v1

--- a/solution.py
+++ b/solution.py
@@ -20,7 +20,7 @@
     fields,
     spaces,
     wiener,
-    inp,
+    given,
     motion,
     spread,
     blend,
@@ -31,7 +31,9 @@
     prefactor,
     ignition,
     out,
+    current0,
     current1,
+    current2,
     partner_planes,
     chip_half,
     other_sums,
@@ -41,8 +43,7 @@
     blend_g,
     thermal_g,
     arrhenius,
-    left_p,
-    right_p,
+    both_p,
     yield_p,
     column,
     pre_b,
@@ -58,9 +59,10 @@
     halo_send,
     halo_recv,
 ):
-    planes, rows, species, lanes = inp.shape
-    reactions = left_w.shape[0]
-    padded = left_p.shape[0]
+    planes, rows, species, lanes = current0.shape
+    reactions = left_w.shape[1]
+    padded = pre_b.shape[0]
+    stride = planes * rows
     half = rows // 2
     chips = fields // 2
     local_rows = spread.shape[1]
@@ -82,6 +84,12 @@
         )
     for neighbour in (left, right):
         pl.semaphore_signal(barrier, inc=1, device_id={"space": neighbour}, device_id_type=MESH)
+
+    def relayout(t, carry):
+        current0[t // rows, lax.rem(t, rows)] = given[pl.ds(t, species, stride=stride), :]
+        return carry
+
+    lax.fori_loop(0, stride, relayout, 0, unroll=4)
     pl.semaphore_wait(barrier, fields + 1)
 
     def remote(src, dst, send, recv, **to):
@@ -94,7 +102,7 @@
             device_id_type=MESH,
         )
 
-    sources = [inp, current1]
+    sources = [current0, current1]
 
     def pair_copy(step, p):
         return remote(
@@ -144,46 +152,48 @@
             field=lax.rem(me + d, fields),
         )
 
+    def reduce_pair(step, p):
+        pair_copy(step, p).wait_recv()
+        chip_half[step, p] = sources[step][p, mine] + partner_planes[step, p, mine]
+
+    def send_cross(step, p):
+        for d in range(1, chips):
+            cross_copy(step, p, d).start()
+
+    def relay(step, p):
+        for d in range(1, chips):
+            cross_copy(step, p, d).wait_recv()
+            relay_copy(step, p, d).start()
+
     pair_copy(0, order[0]).start()
-    for k in range(4):
+    for d in range(1, fields):
+        flow_copy(0, d).start()
+    for p in order[1:]:
+        pair_copy(0, p).start()
+    for k in range(1, 4):
         for d in range(1, fields):
             flow_copy(k, d).start()
-    for p in order[1:]:
-        pair_copy(0, p).start()
     for side in range(2):
         halo_copy(0, side).start()
     for src, dst in flow_pairs:
         dst[me] = src[...]
 
-    left_p[...] = jnp.zeros_like(left_p)
-    right_p[...] = jnp.zeros_like(right_p)
+    reduce_pair(0, order[0])
+    column[...] = jnp.zeros_like(column)
+    for k, src in enumerate((left_w, right_w)):
+        column[0:species, 0:reactions] = src[...].astype(jnp.float32)
+        turned = jnp.transpose(column[...])
+        both_p[k * padded : (k + 1) * padded, :] = turned[0:padded, 0:species].astype(jnp.bfloat16)
     yield_p[...] = jnp.zeros_like(yield_p)
-    left_p[0:reactions, :] = left_w[...]
-    right_p[0:reactions, :] = right_w[...]
     yield_p[:, 0:reactions] = yield_w[...]
+    send_cross(0, order[0])
     for src, dst in ((prefactor, pre_b), (ignition, ign_b)):
-        column[...] = jnp.zeros_like(column)
         column[0:1, 0:reactions] = src[...]
-        spread_rows = jnp.broadcast_to(column[0:1, :], (lanes, column.shape[1]))
-        dst[...] = jnp.transpose(spread_rows)[0:padded, :]
-
-    def reduce_pair(step, p):
-        pair_copy(step, p).wait_recv()
-        chip_half[step, p] = sources[step][p, mine] + partner_planes[step, p, mine]
-
-    def send_cross(step, p):
-        for d in range(1, chips):
-            cross_copy(step, p, d).start()
-
-    def relay(step, p):
-        for d in range(1, chips):
-            cross_copy(step, p, d).wait_recv()
-            relay_copy(step, p, d).start()
-
-    for i, p in enumerate(order):
+        dst[...] = jnp.transpose(jnp.broadcast_to(column[0:1, :], column.shape))[0:padded, :]
+    for i, p in enumerate(order[1:]):
         reduce_pair(0, p)
         if i > 0:
-            send_cross(0, order[i - 1])
+            send_cross(0, order[i])
     for k in range(4):
         for d in range(1, fields):
             flow_copy(k, d).wait_recv()
@@ -232,21 +242,29 @@
 
     def chemistry(p, first, last, dst):
         def one(substep, carry):
+            def settle(base, block, rates):
+                block = block + chem_step * jnp.dot(
+                    yield_p[:, 0:padded], rates, preferred_element_type=jnp.float32
+                )
+                for i in range(TILE_ROWS):
+                    dst[p, base + i] = block[:, i * lanes : (i + 1) * lanes]
+
+            pending = None
             for base in range(0, rows, TILE_ROWS):
                 block = jnp.concatenate([dst[p, base + i] for i in range(TILE_ROWS)], axis=1)
-                low = block.astype(jnp.bfloat16)
-                forward = jnp.dot(left_p[...], low, preferred_element_type=jnp.float32)
-                backward = jnp.dot(right_p[...], low, preferred_element_type=jnp.float32)
+                factors = jnp.dot(
+                    both_p[...], block.astype(jnp.bfloat16), preferred_element_type=jnp.float32
+                )
+                forward, backward = factors[:padded], factors[padded:]
                 level = jnp.concatenate(
                     [arrhenius[p * rows + base + i] for i in range(TILE_ROWS)], axis=1
                 )
                 saturation = 1.0 + forward * forward + backward * backward
                 rates = (level * forward * backward / saturation).astype(jnp.bfloat16)
-                block = block + chem_step * jnp.dot(
-                    yield_p[:, 0:padded], rates, preferred_element_type=jnp.float32
-                )
-                for i in range(TILE_ROWS):
-                    dst[p, base + i] = block[:, i * lanes : (i + 1) * lanes]
+                if pending is not None:
+                    settle(*pending)
+                pending = (base, block, rates)
+            settle(*pending)
             return carry
 
         lax.fori_loop(first, last, one, 0)
@@ -261,7 +279,7 @@
     for k in range(STEPS * planes):
         step, i = divmod(k, planes)
         p = order[i]
-        dst = current1 if step < STEPS - 1 else out
+        dst = current1 if step < STEPS - 1 else current2
         for d in range(1, chips):
             relay_copy(step, p, d).wait_recv()
         if p == 0:
@@ -279,6 +297,13 @@
         chemistry(p, middle, SUB, dst)
         if 1 <= k < planes + 1:
             send_cross(1, order[k - 1])
+        if step == STEPS - 1:
+
+            def finish(y, carry):
+                out[pl.ds(p * rows + y, species, stride=stride), :] = current2[p, y]
+                return carry
+
+            lax.fori_loop(0, rows, finish, 0, unroll=4)
         if step == 0:
             pair_copy(1, p).start()
             if p == planes - 1:
@@ -323,13 +348,15 @@
     others = max(chips - 1, 1)
     f32 = jnp.float32
     vmem = pl.BlockSpec(memory_space=pltpu.VMEM)
-    state = jnp.transpose(composition_vector[0], (1, 2, 0, 3))
+    state = composition_vector.reshape(species * planes * rows, lanes)
     result = pl.pallas_call(
         functools.partial(kernel, fields, spaces),
         out_shape=jax.ShapeDtypeStruct(state.shape, f32),
         in_specs=[pl.BlockSpec(memory_space=pltpu.SMEM)] + [vmem] * 10,
         out_specs=vmem,
         scratch_shapes=[
+            pltpu.VMEM((planes, rows, species, lanes), f32),
+            pltpu.VMEM((planes, rows, species, lanes), f32),
             pltpu.VMEM((planes, rows, species, lanes), f32),
             pltpu.VMEM((STEPS, planes, rows, species, lanes), f32),
             pltpu.VMEM((STEPS, planes, rows // 2, species, lanes), f32),
@@ -340,10 +367,9 @@
             pltpu.VMEM((fields, planes, local_rows, lanes), f32),
             pltpu.VMEM((fields, planes, local_rows, lanes), f32),
             pltpu.VMEM((planes * rows, padded, lanes), f32),
-            pltpu.VMEM((padded, species), jnp.bfloat16),
-            pltpu.VMEM((padded, species), jnp.bfloat16),
+            pltpu.VMEM((2 * padded, species), jnp.bfloat16),
             pltpu.VMEM((species, wide), jnp.bfloat16),
-            pltpu.VMEM((8, wide), f32),
+            pltpu.VMEM((lanes, wide), f32),
             pltpu.VMEM((padded, lanes), f32),
             pltpu.VMEM((padded, lanes), f32),
             pltpu.SemaphoreType.DMA((4, fields)),
@@ -368,13 +394,13 @@
         spreading_strength,
         blend_relax_multiplier,
         thermal_level,
-        left_bilinear_weights,
-        right_bilinear_weights,
+        left_bilinear_weights.T,
+        right_bilinear_weights.T,
         species_yield_weights,
         arrhenius_prefactor[None],
         ignition_energy_ratio[None],
     )
-    return jnp.transpose(result, (2, 0, 1, 3))[None]
+    return result.reshape(composition_vector.shape)
 
 
 def solution(mesh):

time: 78.6 us -> 68 us (0.87)
  local copies, waits for them, and re-layouts: 7.77 us -> 2.31 us
  Pallas kernels: 70.5 us -> 65.5 us
    pallas_call x1, Pallas kernels: 70.5 us -> 65.5 us  [body(): pl.pallas_call(functools.partial(kernel, fields, spaces), out_shape=jax.S...]
    broadcast_in_dim x1 -> x0, local copies, waits for them, and re-layouts: 2.81 us -> none  [body(): return jnp.transpose(result, (2, 0, 1, 3))[None]]
    unnamed x5 -> x1, local copies, waits for them, and re-layouts: 4.96 us -> 2.31 us
where the time goes in v2:
time: 68 us; the launch traced here: 67.9 us
  Pallas kernels  65.5 us (96%)
  local copies, waits for them, and re-layouts  2.31 us (3%)
    pallas_call x1, Pallas kernels, body(): pl.pallas_call(functools.partial(kernel, fields, spaces), out_shape=jax.S...  65.5 us
    unnamed x1, local copies, waits for them, and re-layouts  2.31 us

profile of v2, /device:TPU:0, one launch (start us, length us, event | category | flops | bytes accessed | tf_op | source)
XLA Modules:
  0.0 67.9 jit_solution(5762998287893280981)
XLA Ops:
  0.0 65.5 %fields_step.1 = f32[2048,128]{1,0:T(8,128)} custom-call(f32[2,1,3]{2,1,0:T(1,128)} %wiener.1, f32[2048,128]{1,0:T(8,128)} %bitcast.7, f32[3,4,4,128]{3,2,1,0:T(4,128)} %motion.1, f32[4,4,128]{2,1,0:T(4,128)} %spread.1, f32[4,4,128]{2,1,0:T(4,128)} %blend.1, f32[4,4,128]{2,1,0:T(4,128)} %thermal.1, bf16[32,206]{1,0:T(8,128)(2,1)} %bitcast.8, ...), custom_call_target="tpu_custom_call" | custom-call | tf_op jit(solution)/shard_map/fields_step/pallas_call | solution.py:352
  65.6 2.3 %copy.13 = f32[1,32,4,16,128]{4,3,2,1,0:T(8,128)} copy(f32[1,32,4,16,128]{4,3,2,1,0:T(8,128)} %bitcast.6) | data formatting | bytes 2097152

commit v3 on v2

--- a/solution.py
+++ b/solution.py
@@ -170,9 +170,6 @@
         flow_copy(0, d).start()
     for p in order[1:]:
         pair_copy(0, p).start()
-    for k in range(1, 4):
-        for d in range(1, fields):
-            flow_copy(k, d).start()
     for side in range(2):
         halo_copy(0, side).start()
     for src, dst in flow_pairs:
@@ -187,6 +184,9 @@
     yield_p[...] = jnp.zeros_like(yield_p)
     yield_p[:, 0:reactions] = yield_w[...]
     send_cross(0, order[0])
+    for k in range(1, 4):
+        for d in range(1, fields):
+            flow_copy(k, d).start()
     for src, dst in ((prefactor, pre_b), (ignition, ign_b)):
         column[0:1, 0:reactions] = src[...]
         dst[...] = jnp.transpose(jnp.broadcast_to(column[0:1, :], column.shape))[0:padded, :]
@@ -194,9 +194,8 @@
         reduce_pair(0, p)
         if i > 0:
             send_cross(0, order[i])
-    for k in range(4):
-        for d in range(1, fields):
-            flow_copy(k, d).wait_recv()
+    for d in range(1, fields):
+        flow_copy(0, d).wait_recv()
     send_cross(0, order[-1])
 
     def arrhenius_rows(p):
@@ -274,11 +273,15 @@
     relay(0, order[0])
     for p in order[1:]:
         arrhenius_rows(p)
+    for k in range(1, 4):
+        for d in range(1, fields):
+            flow_copy(k, d).wait_recv()
 
     middle = SUB // 2
+    late_order = list(range(1, planes - 1)) + [planes - 1, 0]
     for k in range(STEPS * planes):
         step, i = divmod(k, planes)
-        p = order[i]
+        p = order[i] if step == 0 else late_order[i]
         dst = current1 if step < STEPS - 1 else current2
         for d in range(1, chips):
             relay_copy(step, p, d).wait_recv()
@@ -288,15 +291,17 @@
             halo_copy(step, 1).wait_recv()
         transport(step, p, dst)
         chemistry(p, 0, middle, dst)
+        if 1 <= k < planes + 1:
+            reduce_pair(1, order[k - 1])
         if k < planes - 1:
             relay(0, order[k + 1])
-        if 2 <= k < planes + 2:
-            relay(1, order[k - 2])
-        if 1 <= k < planes + 1:
-            reduce_pair(1, order[k - 1])
-        chemistry(p, middle, SUB, dst)
+        if 3 <= k < planes + 2:
+            relay(1, order[k - 3])
         if 1 <= k < planes + 1:
             send_cross(1, order[k - 1])
+        if k == planes + 1:
+            relay(1, order[planes - 1])
+        chemistry(p, middle, SUB, dst)
         if step == STEPS - 1:
 
             def finish(y, carry):

time: 68 us -> 60.7 us (0.89)
  Pallas kernels: 65.5 us -> 58 us
    pallas_call x1, Pallas kernels: 65.5 us -> 58 us  [body(): pl.pallas_call(functools.partial(kernel, fields, spaces), out_shape=jax.S...]
where the time goes in v3:
time: 60.7 us; the launch traced here: 60.3 us
  Pallas kernels  58 us (96%)
  local copies, waits for them, and re-layouts  2.31 us (4%)
    pallas_call x1, Pallas kernels, body(): pl.pallas_call(functools.partial(kernel, fields, spaces), out_shape=jax.S...  58 us
    unnamed x1, local copies, waits for them, and re-layouts  2.31 us

profile of v3, /device:TPU:0, one launch (start us, length us, event | category | flops | bytes accessed | tf_op | source)
XLA Modules:
  0.0 60.3 jit_solution(4327576583441622594)
XLA Ops:
  0.0 58.0 %fields_step.1 = f32[2048,128]{1,0:T(8,128)} custom-call(f32[2,1,3]{2,1,0:T(1,128)} %wiener.1, f32[2048,128]{1,0:T(8,128)} %bitcast.7, f32[3,4,4,128]{3,2,1,0:T(4,128)} %motion.1, f32[4,4,128]{2,1,0:T(4,128)} %spread.1, f32[4,4,128]{2,1,0:T(4,128)} %blend.1, f32[4,4,128]{2,1,0:T(4,128)} %thermal.1, bf16[32,206]{1,0:T(8,128)(2,1)} %bitcast.8, ...), custom_call_target="tpu_custom_call" | custom-call | tf_op jit(solution)/shard_map/fields_step/pallas_call | solution.py:357
  58.0 2.3 %copy.13 = f32[1,32,4,16,128]{4,3,2,1,0:T(8,128)} copy(f32[1,32,4,16,128]{4,3,2,1,0:T(8,128)} %bitcast.6) | data formatting | bytes 2097152
